TPU v7x, 32 devices: a whole 2x2x4 slice. The times are simulated.
32 devices in a mesh: ctx: 8 (over z, x), head: 4 (over y, core).
Axes of the slice: x: 2, y: 2, z: 4, core: 2. Of those that a mesh axis runs over, the one named last changes fastest.
Arguments:
- tokens: bfloat16 [16, 8192], P(None, 'ctx'), may hold values from -1000 to 1000
- norm_gain: float32 [8192], P('ctx'), may hold values from 0.5 to 2
- w_query: bfloat16 [8192, 4096], P('ctx', 'head'), may hold values from -0.0625 to 0.0625
- w_out: bfloat16 [4096, 8192], P('head', 'ctx'), may hold values from -0.09375 to 0.09375
- kv_cache: bfloat16 [16, 4, 128, 64, 256], P(None, 'head', 'ctx'), may hold values from -128 to 128
- page_ids: int32 [2, 16, 4, 32], P(None, None, 'head'), may hold values from 0 to 127, as said below
Outputs:
- block_outputs: bfloat16 [2, 16, 8192], P(None, None, 'ctx')
Inputs may be any that keep to these rules, and one draw needn't show every extreme that they name: `page_ids`: entries 0 to 15 and 16 to 31 of each list are its two halves. The 32 pages of one list are distinct. Block b holds pages b * 16 to (b + 1) * 16 - 1; within one half at most 2 pages lie in one block, and every half has exactly 2 pages in some block.
All inputs are finite; a program needn't handle non-finite values.
Results may differ from a plain program's by a relative error of at most 0.019.
Values may be sent and summed in bfloat16 or wider, within the bound.
A program may use at most 64 MiB of HBM per device.

v0:
```python
import functools
import math

import jax
import jax.numpy as jnp
from jax import lax
from jax.experimental import pallas as pl
from jax.experimental.pallas import tpu as pltpu
from jax.sharding import PartitionSpec as P

def ORDER(n):
    return sorted(range(1, n), key=lambda k: (abs(2 * k - n), k))


MESH = pl.DeviceIdType.MESH
HALVES = 2
MOST = 2
SLOTS = HALVES * MOST
PARTS = 2
EPSILON = 1e-05
LOWEST = -1e30


def fold(value):
    span = value.shape[1] // PARTS
    return jnp.concatenate([value[:, p * span : (p + 1) * span] for p in range(PARTS)], axis=0)


def unfold(value):
    band = value.shape[0] // PARTS
    return jnp.concatenate([value[p * band : (p + 1) * band] for p in range(PARTS)], axis=1)


def kernel(
    ctx_count, head_count, steps, rows, heads, hd, page, pages_dev,
    ids_hbm, tokens_hbm, gain_hbm, wq_hbm, wo_hbm, kv_hbm, out_ref,
    ids_ref, tokens_ref, gain_ref, wq, wo, kv, slot_rows, slots, q_all, o_all, c_all, square_all, stat_all, q_rows, o_rows, peak_rows, sum_rows, x_ref,
    load_sems, send_sems, recv_sems,
):
    ctx = lax.axis_index("ctx")
    head = lax.axis_index("head")
    width = tokens_ref.shape[1]
    model_width = width * ctx_count
    feats = heads * hd
    band = rows // PARTS
    f32, bf16 = jnp.float32, jnp.bfloat16

    load_q = pltpu.make_async_copy(wq_hbm, wq, load_sems.at[0])
    load_kv = pltpu.make_async_copy(kv_hbm, kv, load_sems.at[1])
    load_o = pltpu.make_async_copy(wo_hbm, wo, load_sems.at[2])
    load_slots = pltpu.make_async_copy(slot_rows, slots, load_sems.at[3])
    load_tokens = pltpu.make_async_copy(tokens_hbm, tokens_ref, load_sems.at[4])
    load_gain = pltpu.make_async_copy(gain_hbm, gain_ref, load_sems.at[5])
    load_ids = pltpu.make_async_copy(ids_hbm, ids_ref, load_sems.at[6])
    load_tokens.start()
    load_gain.start()
    load_ids.start()
    load_q.start()

    def ctx_peer(k):
        return lax.rem(ctx + k, ctx_count)

    def head_peer(k):
        return lax.rem(head + k, head_count)

    barrier = pltpu.get_barrier_semaphore()
    for k in ORDER(ctx_count):
        pl.semaphore_signal(barrier, inc=1, device_id=(ctx_peer(k), head), device_id_type=MESH)
    for k in range(1, head_count):
        pl.semaphore_signal(barrier, inc=1, device_id=(ctx, head_peer(k)), device_id_type=MESH)

    load_ids.wait()
    ids = ids_ref[...].reshape(steps * rows, ids_ref.shape[3])
    local = ids - ctx * pages_dev
    none = jnp.int32(2 * pages_dev)
    left = jnp.where((local >= 0) & (local < pages_dev), local, none)
    field = lax.broadcasted_iota(jnp.int32, (steps * rows, 128), 1)
    found = jnp.zeros((steps * rows, 128), jnp.int32)
    count = jnp.zeros((steps * rows, 1), jnp.int32)
    for s in range(SLOTS):
        least = jnp.min(left, axis=1, keepdims=True)
        found = jnp.where((field == s) & (least < none), least, found)
        count = count + (least < none).astype(jnp.int32)
        left = jnp.where(left > least, left, none)
    slot_rows[...] = jnp.where(field == SLOTS, count, found)
    load_slots.start()

    def ctx_copy(held, phase, step, part, k):
        return pltpu.make_async_remote_copy(
            src_ref=held.at[step, part, ctx],
            dst_ref=held.at[step, part, ctx],
            send_sem=send_sems.at[step, phase, part],
            recv_sem=recv_sems.at[step, phase, part],
            device_id=(ctx_peer(k), head),
            device_id_type=MESH,
        )

    def head_copy(step, part, k):
        return pltpu.make_async_remote_copy(
            src_ref=c_all.at[step, part, head],
            dst_ref=c_all.at[step, part, head],
            send_sem=send_sems.at[step, 2, part],
            recv_sem=recv_sems.at[step, 2, part],
            device_id=(ctx, head_peer(k)),
            device_id_type=MESH,
        )

    def arrived(held, phase, step, part, others):
        ref = held.at[step, part, pl.ds(0, others)]
        pltpu.make_async_copy(ref, ref, recv_sems.at[step, phase, part]).wait()

    lane = lax.broadcasted_iota(jnp.int32, (band, 128), 1)
    row = lax.broadcasted_iota(jnp.int32, (band, 128), 0)
    token = lax.broadcasted_iota(jnp.int32, (heads, SLOTS * page), 1)

    def take_step(step, part):
        span = slice(part * band, (part + 1) * band)
        if step == 0:
            x = tokens_ref[...].astype(f32)[span]
        else:
            block = head_sum(step - 1, part)
            x = (x_ref[span, :] + block).astype(bf16).astype(f32)
        x_ref[span, :] = x
        squares = jnp.sum(x * x, axis=1, keepdims=True)
        square_all[step, part, ctx] = jnp.sum(jnp.where(lane == row, squares, 0.0), axis=0, keepdims=True)
        if step == 0 and part == 0:
            load_q.wait()
            load_kv.start()
            load_o.start()
        scaled = (x * gain_ref[...]).astype(bf16)
        partial = jnp.dot(scaled, wq[...], preferred_element_type=f32)
        q_all[step, part, ctx] = fold(partial).astype(bf16)
        if step == 0 and part == 0:
            pl.semaphore_wait(barrier, ctx_count + head_count - 2)
        for k in ORDER(ctx_count):
            ctx_copy(square_all, 3, step, part, k).start()
        for k in ORDER(ctx_count):
            ctx_copy(q_all, 0, step, part, k).start()

    def head_sum(step, part):
        arrived(c_all, 2, step, part, head_count - 1)
        total = c_all[step, part, 0].astype(f32)
        for k in range(1, head_count):
            total = total + c_all[step, part, k].astype(f32)
        block = unfold(total).astype(bf16)
        out_ref[step, part * band : (part + 1) * band, :] = block
        return block.astype(f32)

    def attend(step, part):
        arrived(square_all, 3, step, part, ctx_count - 1)
        square = square_all[step, part, 0]
        for k in ORDER(ctx_count):
            square = square + square_all[step, part, k]
        square = jnp.sum(jnp.where(lane == row, square, 0.0), axis=1, keepdims=True)
        inv_rms = 1.0 / jnp.sqrt(square / model_width + EPSILON)
        arrived(q_all, 0, step, part, ctx_count - 1)
        total = q_all[step, part, 0].astype(f32)
        for k in ORDER(ctx_count):
            total = total + q_all[step, part, k].astype(f32)
        query = (unfold(total) * inv_rms).astype(bf16).astype(f32)
        for h in range(heads):
            q_rows[part, h * band : (h + 1) * band, :] = query[:, h * hd : (h + 1) * hd]
        if step == 0 and part == 0:
            load_slots.wait()
            load_kv.wait()
        values = []
        all_weights = []
        all_scores = []
        for i in range(band):
            r = part * band + i
            at = step * rows + r
            both = jnp.concatenate([kv[r, slots[at, s]] for s in range(SLOTS)], axis=0)
            values.append(both[:, hd:])
            scores = lax.dot_general(
                q_rows[part, pl.ds(i, heads, stride=band), :].astype(bf16), both[:, :hd],
                (((1,), (1,)), ((), ())), preferred_element_type=f32,
            ) * (1.0 / math.sqrt(hd))
            all_scores.append(jnp.where(token < slots[at, SLOTS] * page, scores, -jnp.inf))
        for i in range(band):
            peak = jnp.maximum(jnp.max(all_scores[i], axis=1, keepdims=True), LOWEST)
            weights = jnp.exp(all_scores[i] - peak)
            all_weights.append(weights.astype(bf16))
            peak_rows[part, pl.ds(i, heads, stride=band), :] = jnp.broadcast_to(peak, (heads, 128))
            sum_rows[part, pl.ds(i, heads, stride=band), :] = jnp.broadcast_to(
                jnp.sum(weights, axis=1, keepdims=True), (heads, 128)
            )
        for i in range(band):
            o_rows[part, pl.ds(i, heads, stride=band), :] = jnp.dot(
                all_weights[i], values[i], preferred_element_type=f32
            )
        stats = jnp.zeros((band, 128), f32)
        pieces = []
        for h in range(heads):
            span = slice(h * band, (h + 1) * band)
            pieces.append(o_rows[part, span, :])
            stats = jnp.where(lane == row * heads + h, peak_rows[part, span, :], stats)
            stats = jnp.where(lane == band * heads + row * heads + h, sum_rows[part, span, :], stats)
        stat_all[step, part, ctx] = jnp.sum(stats, axis=0, keepdims=True)
        o_all[step, part, ctx] = fold(jnp.concatenate(pieces, axis=1)).astype(bf16)
        for k in ORDER(ctx_count):
            ctx_copy(stat_all, 4, step, part, k).start()
        for k in ORDER(ctx_count):
            ctx_copy(o_all, 1, step, part, k).start()

    def project(step, part):
        arrived(stat_all, 4, step, part, ctx_count - 1)
        stats = [stat_all[step, part, k] for k in range(ctx_count)]
        top = functools.reduce(jnp.maximum, stats)
        factors = [jnp.exp(jnp.where(lane[:1] < band * heads, stat - top, 0.0)) for stat in stats]
        below = sum(f * pltpu.roll(stat, 128 - band * heads, 1) for f, stat in zip(factors, stats))
        shares = [jnp.broadcast_to(f / below, (band, 128)) for f in factors]
        arrived(o_all, 1, step, part, ctx_count - 1)
        parts = [unfold(o_all[step, part, k].astype(f32)) for k in range(ctx_count)]
        mixed = []
        for h in range(heads):
            span = slice(h * hd, (h + 1) * hd)
            mine = lane == row * heads + h
            mixed.append(
                sum(
                    jnp.sum(jnp.where(mine, shares[k], 0.0), axis=1, keepdims=True) * parts[k][:, span]
                    for k in range(ctx_count)
                )
            )
        attn = jnp.concatenate(mixed, axis=1).astype(bf16)
        if step == 0 and part == 0:
            load_o.wait()
        c_all[step, part, head] = fold(jnp.dot(attn, wo[...], preferred_element_type=f32)).astype(bf16)
        for k in range(1, head_count):
            head_copy(step, part, k).start()

    load_tokens.wait()
    load_gain.wait()
    for step in range(steps):
        for part in range(PARTS):
            take_step(step, part)
        for part in range(PARTS):
            attend(step, part)
        for part in range(PARTS):
            project(step, part)
    for part in range(PARTS):
        head_sum(steps - 1, part)

    for step in range(steps):
        for part in range(PARTS):
            for k in ORDER(ctx_count):
                ctx_copy(q_all, 0, step, part, k).wait_send()
                ctx_copy(o_all, 1, step, part, k).wait_send()
                ctx_copy(square_all, 3, step, part, k).wait_send()
                ctx_copy(stat_all, 4, step, part, k).wait_send()
            for k in range(1, head_count):
                head_copy(step, part, k).wait_send()


def shards(ctx_count, head_count, tokens, norm_gain, w_query, w_out, kv_cache, page_ids):
    rows, width = tokens.shape
    steps = page_ids.shape[0]
    _, _, pages_dev, page, both = kv_cache.shape
    hd = both // 2
    heads = w_query.shape[1] // hd
    band = rows // PARTS
    sent = heads * hd // PARTS
    vmem = pl.BlockSpec(memory_space=pltpu.VMEM)
    hbm = pl.BlockSpec(memory_space=pl.ANY)
    bf16, f32 = jnp.bfloat16, jnp.float32
    return pl.pallas_call(
        functools.partial(kernel, ctx_count, head_count, steps, rows, heads, hd, page, pages_dev),
        out_shape=jax.ShapeDtypeStruct((steps, rows, width), bf16),
        in_specs=[hbm] * 6,
        out_specs=vmem,
        scratch_shapes=[
            pltpu.VMEM(page_ids.shape, jnp.int32),
            pltpu.VMEM((rows, width), bf16),
            pltpu.VMEM((1, width), f32),
            pltpu.VMEM(w_query.shape, bf16),
            pltpu.VMEM(w_out.shape, bf16),
            pltpu.VMEM((rows, pages_dev, page, both), bf16),
            pltpu.VMEM((steps * rows, 128), jnp.int32),
            pltpu.SMEM((steps * rows, 128), jnp.int32),
            pltpu.VMEM((steps, PARTS, ctx_count, rows, sent), bf16),
            pltpu.VMEM((steps, PARTS, ctx_count, rows, sent), bf16),
            pltpu.VMEM((steps, PARTS, head_count, rows, width // PARTS), bf16),
            pltpu.VMEM((steps, PARTS, ctx_count, 1, 128), f32),
            pltpu.VMEM((steps, PARTS, ctx_count, 1, 128), f32),
            pltpu.VMEM((PARTS, heads * band, hd), f32),
            pltpu.VMEM((PARTS, heads * band, hd), f32),
            pltpu.VMEM((PARTS, heads * band, 128), f32),
            pltpu.VMEM((PARTS, heads * band, 128), f32),
            pltpu.VMEM((rows, width), f32),
            pltpu.SemaphoreType.DMA((7,)),
            pltpu.SemaphoreType.DMA((steps, 5, PARTS)),
            pltpu.SemaphoreType.DMA((steps, 5, PARTS)),
        ],
        compiler_params=pltpu.CompilerParams(
            collective_id=0, has_side_effects=True, vmem_limit_bytes=56 * 1024 * 1024
        ),
    )(
        page_ids, tokens, norm_gain.reshape(1, width), w_query, w_out,
        kv_cache.reshape(rows, pages_dev, page, both),
    )


def solution(mesh):
    placed = (
        P(None, "ctx"),
        P("ctx"),
        P("ctx", "head"),
        P("head", "ctx"),
        P(None, "head", "ctx", None, None),
        P(None, None, "head", None),
    )
    return jax.shard_map(
        functools.partial(shards, mesh.shape["ctx"], mesh.shape["head"]),
        mesh=mesh, in_specs=placed, out_specs=P(None, None, "ctx"), check_vma=False,
    )
```

profile of v0, /device:TPU:0, one launch (start us, length us, event | category | flops | bytes accessed | tf_op | source)
XLA Modules:
  0.0 41.0 jit_solution(4898451776287089236)
XLA Ops:
  0.0 39.5 %shard_map.64 = bf16[2,16,1024]{2,1,0:T(8,128)(2,1)} custom-call(s32[2,16,1,32]{3,2,1,0:T(1,128)} %ids_hbm.1, bf16[16,1024]{1,0:T(8,128)(2,1)} %tokens_hbm.1, f32[1,1024]{1,0:T(1,128)} %bitcast.3, bf16[1024,1024]{1,0:T(8,128)(2,1)} %wq_hbm.1, bf16[1024,1024]{1,0:T(8,128)(2,1)} %wo_hbm.1, bf16[16,16,64,256]{3,2,1,0:T(8,128)(2,1)} %bitcast.2), custom_call_target="tpu_custom_call" | custom-call | tf_op jit(solution)/shard_map/pallas_call | solution.py:265
  39.5 1.5 %copy.8 = bf16[2,16,1024]{2,1,0:T(8,128)(2,1)} copy(bf16[2,16,1024]{2,1,0:T(8,128)(2,1)} %shard_map.64) | data formatting | bytes 131072
where the time goes:
time: 41.1 us; the launch traced here: 41 us
  Pallas kernels  39.5 us (96%)
  local copies, waits for them, and re-layouts  1.47 us (4%)
    pallas_call x1, Pallas kernels, shards(): pl.pallas_call(functools.partial(kernel, ctx_count, head_count, steps, ro...  39.5 us
    unnamed x1, local copies, waits for them, and re-layouts  1.47 us

commit v1 on v0

--- a/solution.py
+++ b/solution.py
@@ -291,11 +291,16 @@
             pltpu.SemaphoreType.DMA((steps, 5, PARTS)),
         ],
         compiler_params=pltpu.CompilerParams(
-            collective_id=0, has_side_effects=True, vmem_limit_bytes=56 * 1024 * 1024
+            collective_id=0, has_side_effects=True, vmem_limit_bytes=40 * 1024 * 1024
         ),
     )(
-        page_ids, tokens, norm_gain.reshape(1, width), w_query, w_out,
-        kv_cache.reshape(rows, pages_dev, page, both),
+        *(
+            pltpu.with_memory_space_constraint(operand, pltpu.HBM)
+            for operand in (
+                page_ids, tokens, norm_gain.reshape(1, width), w_query, w_out,
+                kv_cache.reshape(rows, pages_dev, page, both),
+            )
+        )
     )
 
 

time: 41.1 us -> 39.7 us (0.966)
  local copies, waits for them, and re-layouts: 1.47 us -> 0.63 us
  Pallas kernels: 39.5 us -> 38.9 us
    unnamed x1, local copies, waits for them, and re-layouts: 1.47 us -> 0.63 us
    pallas_call x1, Pallas kernels: 39.5 us -> 38.9 us  [shards(): pl.pallas_call(functools.partial(kernel, ctx_count, head_count, steps, ro...]
where the time goes in v1:
time: 39.7 us; the launch traced here: 39.5 us
  Pallas kernels  38.9 us (98%)
  local copies, waits for them, and re-layouts  0.63 us (2%)
    pallas_call x1, Pallas kernels, shards(): pl.pallas_call(functools.partial(kernel, ctx_count, head_count, steps, ro...  38.9 us

profile of v1, /device:TPU:0, one launch (start us, length us, event | category | flops | bytes accessed | tf_op | source)
XLA Modules:
  0.0 39.5 jit_solution(1149704346153218958)
XLA Ops:
  0.0 38.9 %shard_map.64 = bf16[2,16,1024]{2,1,0:T(8,128)(2,1)S(1)} custom-call(s32[2,16,1,32]{3,2,1,0:T(1,128)} %ids_hbm.1, bf16[16,1024]{1,0:T(8,128)(2,1)} %tokens_hbm.1, f32[1,1024]{1,0:T(1,128)} %bitcast.3, bf16[1024,1024]{1,0:T(8,128)(2,1)} %wq_hbm.1, bf16[1024,1024]{1,0:T(8,128)(2,1)} %wo_hbm.1, bf16[16,16,64,256]{3,2,1,0:T(8,128)(2,1)} %bitcast.2), custom_call_target="tpu_custom_call" | custom-call | tf_op jit(solution)/shard_map/pallas_call | solution.py:265
  38.9 0.6 %copy.8 = bf16[2,16,1024]{2,1,0:T(8,128)(2,1)} copy(bf16[2,16,1024]{2,1,0:T(8,128)(2,1)S(1)} %shard_map.64) | data formatting | bytes 131072
